TPU v7x, 256 devices: a whole 4x4x8 slice. The times are simulated.
256 devices in a mesh: dp: 8 (over z), expert: 32 (over y, x, core).
Axes of the slice: x: 4, y: 4, z: 8, core: 2. Of those that a mesh axis runs over, the one named last changes fastest.
Arguments:
- activations: bfloat16 [131072, 1024], P(('dp', 'expert')), may hold values from -6 to 6
- out_grad: bfloat16 [131072, 1024], P(('dp', 'expert')), may hold values from -1.5 to 1.5
- w_in: bfloat16 [1024, 64, 1024], P('dp', 'expert'), may hold values from -0.1875 to 0.1875
- w_out: bfloat16 [1024, 64, 1024], P('dp', 'expert'), may hold values from -0.1875 to 0.1875
- token_lists: int32 [8, 64, 512], P('dp', 'expert'), may hold values from 0 to 16383, as said below
- valid_mask: int32 [8, 64, 512], P('dp', 'expert'), may hold values from 0 to 1, as said below
- gate_weights: float32 [8, 64, 512], P('dp', 'expert'), may hold values from 0.05 to 1
Outputs:
- token_grad: bfloat16 [131072, 1024], P(('dp', 'expert'))
- gate_grad: float32 [8, 64, 512], P('dp', 'expert')
- w_in_grad: bfloat16 [1024, 64, 1024], P('dp', 'expert')
- w_out_grad: bfloat16 [1024, 64, 1024], P('dp', 'expert')
Inputs may be any that keep to these rules, and one draw needn't show every extreme that they name: `token_lists`: entries are token numbers within the data group (its 16384 tokens in the order of the expert axis). Valid entries of one list are distinct; padded entries are 0. Among the valid entries of the 2 lists of one index of the expert axis, at most 48 lie in the 512 tokens of any one index of that axis; in every group some index of the expert axis holds exactly 48 tokens chosen by the lists of every index. `valid_mask`: each list's ones form a prefix of 256 or more entries; some list of every group is full.
All inputs are finite; a program needn't handle non-finite values.
Results may differ from a plain program's by a relative error of at most 0.017.
Values may be sent and summed in bfloat16 or wider, within the bound.
A program may use at most 128 MiB of HBM per device.

v0:
```python
import jax
import jax.numpy as jnp
from jax import lax
from jax.sharding import PartitionSpec as P

gelu_coef = 0.7978845608028654
cubic_coef = 0.044715


def gelu_parts(value):
    inner = gelu_coef * (value + cubic_coef * value * value * value)
    tangent = jnp.tanh(inner)
    result = 0.5 * value * (1.0 + tangent)
    slope = 0.5 * (1.0 + tangent) + 0.5 * value * (1.0 - tangent * tangent) * gelu_coef * (
        1.0 + 3.0 * cubic_coef * value * value
    )
    return (result, slope)


def expert_chain(picked_in, picked_grad, gates, apply_in, apply_out, return_out, return_in):
    pre_act = apply_in(picked_in)
    hidden, slope = gelu_parts(pre_act)
    hidden = hidden.astype(jnp.bfloat16)
    expert_out = apply_out(hidden)
    gate_grad = jnp.sum(picked_grad.astype(jnp.float32) * expert_out, axis=-1)
    scaled = (gates[:, :, None] * picked_grad).astype(jnp.bfloat16)
    hidden_grad = return_out(scaled)
    pre_grad = (hidden_grad * slope).astype(jnp.bfloat16)
    in_grad = return_in(pre_grad).astype(jnp.bfloat16)
    return (hidden, scaled, pre_grad, in_grad, gate_grad)


def on_device(activations, out_grad, w_in, w_out, token_lists, valid_mask, gate_weights):
    n_peers = lax.axis_size("expert")
    tok_local = activations.shape[0]
    width = activations.shape[1]
    exp_local = token_lists.shape[1]
    cap_len = token_lists.shape[2]
    picks = exp_local * cap_len
    slots = max(2, 3 * picks // (2 * n_peers))
    flat_lists = token_lists.reshape(picks)
    live = valid_mask.reshape(picks) == 1
    owners = flat_lists // tok_local
    peers = jnp.arange(n_peers, dtype=jnp.int32)
    hits = ((owners[:, None] == peers[None, :]) & live[:, None]).astype(jnp.int32)
    before = jnp.sum((jnp.cumsum(hits, axis=0) - hits) * hits, axis=1)
    slot_of = jnp.where(live, owners * slots + before, n_peers * slots)
    table = (
        jnp.full((n_peers * slots,), -1, jnp.int32)
        .at[slot_of]
        .set(flat_lists % tok_local, mode="drop")
    )
    wanted = lax.all_to_all(
        table.reshape(n_peers, slots), "expert", split_axis=0, concat_axis=0, tiled=True
    )
    present = wanted >= 0
    source = jnp.where(present, wanted, 0)
    outgoing = jnp.stack([activations[source], out_grad[source]], axis=2)
    outgoing = jnp.where(present[:, :, None, None], outgoing, jnp.zeros((), jnp.bfloat16))
    arrived = lax.all_to_all(outgoing, "expert", split_axis=0, concat_axis=0, tiled=True)
    safe_slot = jnp.minimum(slot_of, n_peers * slots - 1)
    gathered = arrived.reshape(n_peers * slots, 2, width)[safe_slot]
    gathered = jnp.where(live[:, None, None], gathered, jnp.zeros((), jnp.bfloat16))
    picked_in = gathered[:, 0].reshape(exp_local, cap_len, width)
    picked_grad = gathered[:, 1].reshape(exp_local, cap_len, width)
    gates = (gate_weights * valid_mask.astype(jnp.float32)).reshape(exp_local, cap_len)
    full_in, full_out = (
        lax.all_gather(w_in, "dp", axis=0, tiled=True),
        lax.all_gather(w_out, "dp", axis=0, tiled=True),
    )

    def apply_in(rows):
        return jnp.einsum("ecd,def->ecf", rows, full_in, preferred_element_type=jnp.float32)

    def apply_out(rows):
        return jnp.einsum("ecf,fed->ecd", rows, full_out, preferred_element_type=jnp.float32)

    def return_out(rows):
        return jnp.einsum("ecd,fed->ecf", rows, full_out, preferred_element_type=jnp.float32)

    def return_in(rows):
        return jnp.einsum("ecf,def->ecd", rows, full_in, preferred_element_type=jnp.float32)

    hidden, scaled, pre_grad, in_grad, gate_grad = expert_chain(
        picked_in, picked_grad, gates, apply_in, apply_out, return_out, return_in
    )
    part = picked_in
    w_in_grad = lax.psum_scatter(
        jnp.einsum("ecd,ecf->def", part, pre_grad, preferred_element_type=jnp.float32).astype(
            jnp.bfloat16
        ),
        "dp",
        scatter_dimension=0,
        tiled=True,
    )
    part = hidden
    w_out_grad = lax.psum_scatter(
        jnp.einsum("ecf,ecd->fed", part, scaled, preferred_element_type=jnp.float32).astype(
            jnp.bfloat16
        ),
        "dp",
        scatter_dimension=0,
        tiled=True,
    )
    back_rows = (
        jnp.zeros((n_peers * slots, width), jnp.bfloat16)
        .at[slot_of]
        .set(in_grad.reshape(picks, width), mode="drop")
    )
    returned = lax.all_to_all(
        back_rows.reshape(n_peers, slots, width), "expert", split_axis=0, concat_axis=0, tiled=True
    )
    token_grad = jax.ops.segment_sum(
        returned.reshape(n_peers * slots, width).astype(jnp.float32),
        source.reshape(-1),
        num_segments=tok_local,
    ).astype(jnp.bfloat16)
    return (token_grad, gate_grad.reshape(1, exp_local, cap_len), w_in_grad, w_out_grad)


def solution(mesh):
    return jax.shard_map(
        on_device,
        mesh=mesh,
        in_specs=(
            P(("dp", "expert"), None),
            P(("dp", "expert"), None),
            P("dp", "expert", None),
            P("dp", "expert", None),
            P("dp", "expert", None),
            P("dp", "expert", None),
            P("dp", "expert", None),
        ),
        out_specs=(
            P(("dp", "expert"), None),
            P("dp", "expert", None),
            P("dp", "expert", None),
            P("dp", "expert", None),
        ),
        check_vma=False,
    )
```

profile of v0, /device:TPU:2, one launch (start us, length us, event | category | flops | bytes accessed | tf_op | source)
XLA Modules:
  0.0 326.2 jit_solution(7288001116280132265)
XLA Ops:
  7.2 2.0 copy.53
  12.8 9.0 %reduce-window.6 = s32[32,8,128]{2,1,0:T(8,128)S(1)} reduce-window(s32[32,8,128]{2,1,0:T(8,128)S(1)} %fusion.17, s32[]{:T(128)} %constant.24.clone.1), window={size=1x1x128 pad=0_0x0_0x127_0}, to_apply=%region_0.1 | reduce-window | flops 4161536 | bytes 262148 | tf_op jit(solution)/shard_map/reduce-window
  22.4 4.3 %scatter_custom_fusion = s32[1536]{0:T(1024)S(1)} fusion(s32[1024]{0:T(1024)S(1)} %bitcast.96, s32[1024]{0:T(1024)S(1)} %get-tuple-element.28, s32[]{:T(128)} %constant.20.clone.1), kind=kCustom, calls=%fused_computation.65 | custom fusion | bytes 6148 | tf_op jit(solution)/shard_map/scatter | solution.py:51
  26.9 13.6 %all_to_all.25 = s32[32,1,48]{2,1,0:T(1,128)S(1)} all-to-all(s32[32,1,48]{2,1,0:T(1,128)S(1)} %all_to_all.16), channel_id=1, replica_groups=mesh['dp'=8,'expert'=32] {'expert'}, dimensions={0} | all-to-all | bytes 12288 | tf_op jit(solution)/shard_map/all_to_all | solution.py:53
  40.5 5.9 %gather_fusion.1 = bf16[1536,1024]{1,0:T(8,128)(2,1)} fusion(bf16[512,1024]{1,0:T(8,128)(2,1)S(1)} %copy-done, s32[2048]{0:T(1024)S(1)} %pad_clamp_fusion), kind=kCustom, calls=%fused_computation.1 | custom fusion | bytes 6297600 | tf_op jit(solution)/shard_map/gather | solution.py:58
  46.4 5.8 %gather_fusion = bf16[1536,1024]{1,0:T(8,128)(2,1)} fusion(bf16[512,1024]{1,0:T(8,128)(2,1)S(1)} %copy-done.2, s32[2048]{0:T(1024)S(1)} %pad_clamp_fusion), kind=kCustom, calls=%fused_computation | custom fusion | bytes 6297600 | tf_op jit(solution)/shard_map/gather | solution.py:58
  52.3 6.6 %maximum_select_fusion = bf16[32,48,2,1024]{3,1,2,0:T(8,128)(2,1)} fusion(bf16[32,48,1,1024]{3,1,2,0:T(8,128)(2,1)} %bitcast.74, bf16[32,48,1,1024]{3,1,2,0:T(8,128)(2,1)} %bitcast.75, pred[32,48]{1,0:T(8,128)(4,1)S(1)} %compare_bitcast_fusion), kind=kLoop, calls=%fused_computation.7 | loop fusion | flops 6291456 | bytes 12584448 | tf_op jit(solution)/shard_map/jit(_where)/select_n | solution.py:59
  58.9 6.1 %all-to-all-start.1 = ((bf16[32,48,2,1024]{3,1,2,0:T(8,128)(2,1)}), bf16[32,48,2,1024]{3,1,2,0:T(8,128)(2,1)}, u32[]{:S(2)}, u32[]{:S(2)}) async-start(bf16[32,48,2,1024]{3,1,2,0:T(8,128)(2,1)} %maximum_select_fusion), calls=%async_computation.1 | async-start | bytes 12582912 | tf_op jit(solution)/shard_map/all_to_all | solution.py:60
  66.3 74.0 %all-to-all-done.1 = bf16[32,48,2,1024]{3,1,2,0:T(8,128)(2,1)} async-done(((bf16[32,48,2,1024]{3,1,2,0:T(8,128)(2,1)}), bf16[32,48,2,1024]{3,1,2,0:T(8,128)(2,1)}, u32[]{:S(2)}, u32[]{:S(2)}) %all-to-all-start.1) | async-done | bytes 6291488 | tf_op jit(solution)/shard_map/all_to_all | solution.py:60
  140.3 12.7 %copy.51 = bf16[32,48,2,1024]{3,2,1,0:T(2,128)(2,1)} copy(bf16[32,48,2,1024]{3,1,2,0:T(8,128)(2,1)} %all-to-all-done.1) | data formatting | bytes 12582912 | tf_op jit(solution)/shard_map/all_to_all | solution.py:60
  153.0 18.5 %gather_fusion.2 = bf16[1024,2,1024]{2,1,0:T(2,128)(2,1)} fusion(bf16[1536,2,1024]{2,1,0:T(2,128)(2,1)} %bitcast.72, s32[1024]{0:T(1024)S(1)} %broadcast_clamp_fusion), kind=kCustom, calls=%fused_computation.2 | custom fusion | bytes 8392704 | tf_op jit(solution)/shard_map/gather | solution.py:62
  171.5 7.9 %broadcast_select_fusion = bf16[1024,2,1024]{2,1,0:T(2,128)(2,1)S(1)} fusion(bf16[1024,2,1024]{2,1,0:T(2,128)(2,1)} %gather_fusion.2, pred[1024]{0:T(1024)(128)(4,1)S(1)} %eq.71), kind=kLoop, calls=%fused_computation.6 | loop fusion | flops 2097152 | bytes 8389632 | tf_op jit(solution)/shard_map/jit(_where)/select_n | solution.py:63
  179.4 5.9 %slice_convert_fusion = (f32[1024,1,1024]{2,1,0:T(1,128)S(1)}, bf16[1024,1,1024]{2,1,0:T(2,128)(2,1)S(1)}) fusion(bf16[1024,2,1024]{2,1,0:T(2,128)(2,1)S(1)} %broadcast_select_fusion), kind=kLoop, calls=%fused_computation.19 | loop fusion | flops 1048576 | bytes 10485760 | tf_op jit(solution)/shard_map/convert_element_type | solution.py:26
  185.3 3.0 copy.68
  189.1 4.7 %fusion.25 = f32[2,512,1024]{2,1,0:T(8,128)S(1)} fusion(bf16[2,512,1024]{2,1,0:T(8,128)(2,1)S(1)} %bitcast.81, bf16[1024,2,1024]{2,0,1:T(8,128)(2,1)} %all-gather.5.cloned.1.call-done), kind=kOutput, calls=%fused_computation.72 | convolution fusion | flops 2147483648 | bytes 10485760 | tf_op jit(solution)/shard_map/ecd,def->ecf/dot_general | solution.py:73
  193.8 4.3 %convolution_convert_fusion = bf16[2,1024,1024]{2,1,0:T(8,128)(2,1)} fusion(f32[2,512,1024]{2,1,0:T(8,128)S(1)} %bitcast.78, f32[2,512]{1,0:T(2,128)S(1)} %multiply_bitcast_fusion, f32[2,512,1024]{2,1,0:T(8,128)S(1)} %fusion.25), kind=kOutput, calls=%fused_computation.23 | convolution fusion | flops 2161115136 | bytes 12587008 | tf_op jit(solution)/shard_map/ecf,ecd->fed/dot_general | solution.py:98
  198.1 6.5 %copy.66 = bf16[1024,2048]{1,0:T(8,128)(2,1)} copy(bf16[1024,2048]{0,1:T(8,128)(2,1)} %bitcast.80) | data formatting | bytes 8388608
  204.9 8.2 %fusion.8 = bf16[2,512,1024]{2,1,0:T(8,128)(2,1)S(1)} fusion(f32[2,512,1024]{2,1,0:T(8,128)} %copy-done.7, bf16[1024,2,1024]{2,0,1:T(8,128)(2,1)} %all-gather.3.cloned.1.call-done, f32[2,512,1024]{2,1,0:T(8,128)} %bitcast.76, f32[2,512]{1,0:T(2,128)S(1)} %multiply_bitcast_fusion), kind=kOutput, calls=%fused_computation.18 | convolution fusion | flops 2169503744 | bytes 14684160 | tf_op jit(solution)/shard_map/ecd,fed->ecf/dot_general | solution.py:79
  213.2 4.4 %convolution_convert_fusion.1 = bf16[2,1024,1024]{2,1,0:T(8,128)(2,1)} fusion(bf16[2,512,1024]{2,1,0:T(8,128)(2,1)S(1)} %fusion.8, bf16[2,512,1024]{2,1,0:T(8,128)(2,1)S(1)} %bitcast.82), kind=kOutput, calls=%fused_computation.24 | convolution fusion | flops 2149580800 | bytes 8388608 | tf_op jit(solution)/shard_map/ecd,ecf->def/dot_general | solution.py:89
  217.6 6.5 %copy.64 = bf16[1024,2048]{1,0:T(8,128)(2,1)} copy(bf16[1024,2048]{0,1:T(8,128)(2,1)} %bitcast.79) | data formatting | bytes 8388608
  224.1 5.3 %convolution_convert_fusion.2 = bf16[2,512,1024]{2,1,0:T(8,128)(2,1)S(1)} fusion(bf16[2,512,1024]{2,1,0:T(8,128)(2,1)} %copy-done.8, bf16[1024,2,1024]{2,0,1:T(8,128)(2,1)} %all-gather.5.cloned.1.call-done), kind=kOutput, calls=%fused_computation.25 | convolution fusion | flops 2148532224 | bytes 8388608 | tf_op jit(solution)/shard_map/ecf,def->ecd/dot_general | solution.py:82
  229.4 7.5 %scatter_custom_fusion.1 = bf16[1536,1024]{1,0:T(8,128)(2,1)} fusion(s32[1024]{0:T(1024)S(1)} %bitcast.97, bf16[1024,1024]{1,0:T(8,128)(2,1)S(1)} %bitcast.98, bf16[]{:T(256)} %constant.54.clone.1), kind=kCustom, calls=%fused_computation.26 | custom fusion | bytes 3145730 | tf_op jit(solution)/shard_map/scatter | solution.py:108
  236.9 7.5 %all-to-all-start.2 = ((bf16[32,48,1024]{2,1,0:T(8,128)(2,1)}), bf16[32,48,1024]{2,1,0:T(8,128)(2,1)}, u32[]{:S(2)}, u32[]{:S(2)}) async-start(bf16[32,48,1024]{2,1,0:T(8,128)(2,1)} %bitcast.73), calls=%async_computation.2 | async-start | bytes 6291456 | tf_op jit(solution)/shard_map/all_to_all | solution.py:110
  245.7 8.2 %multiply_reduce_fusion = f32[2,512]{1,0:T(2,128)} fusion(f32[2,512,1024]{2,1,0:T(8,128)} %bitcast.77, bf16[1024,2,1024]{2,0,1:T(8,128)(2,1)} %all-gather.3.cloned.1.call-done, f32[2,512,1024]{2,1,0:T(8,128)} %copy-done.7), kind=kOutput, calls=%fused_computation.20 | convolution fusion | flops 2159016960 | bytes 12587008 | tf_op jit(solution)/shard_map/ecf,fed->ecd/dot_general | solution.py:76
  253.9 30.3 %all-to-all-done.2 = bf16[32,48,1024]{2,1,0:T(8,128)(2,1)} async-done(((bf16[32,48,1024]{2,1,0:T(8,128)(2,1)}), bf16[32,48,1024]{2,1,0:T(8,128)(2,1)}, u32[]{:S(2)}, u32[]{:S(2)}) %all-to-all-start.2) | async-done | bytes 3145760 | tf_op jit(solution)/shard_map/all_to_all | solution.py:110
  284.2 14.5 %scatter_custom_fusion.2 = f32[512,1024]{1,0:T(8,128)S(1)} fusion(s32[1536]{0:T(1024)S(1)} %fusion.18, bf16[1536,1024]{1,0:T(8,128)(2,1)} %bitcast.24, f32[]{:T(128)} %constant.19.clone.1), kind=kCustom, calls=%fused_computation.8 | custom fusion | flops 3145728 | bytes 5242884 | tf_op jit(solution)/shard_map/scatter-add | solution.py:113
  298.6 1.1 convert_element_type.60
  299.8 1.3 copy.67
  301.1 1.1 copy.57
  302.2 15.0 %reduce-scatter.7.cloned.1.call-done = bf16[128,2048]{1,0:T(8,128)(2,1)} async-done(((bf16[1024,2048]{1,0:T(8,128)(2,1)}), bf16[128,2048]{1,0:T(8,128)(2,1)}) %reduce-scatter.7.cloned.1.call-update) | async-done | bytes 524304
  317.3 1.3 copy.65
  318.6 1.1 copy.56
  (62 shorter events, 8.0 us)
Async XLA Ops:
  7.2 33.4 %copy-start = (bf16[512,1024]{1,0:T(8,128)(2,1)S(1)}, bf16[512,1024]{1,0:T(8,128)(2,1)}, u32[]{:S(2)}) copy-start(bf16[512,1024]{1,0:T(8,128)(2,1)} %param.8) | copy-start | bytes 3145732
  7.2 181.9 %all-gather.5.cloned.1.call-start = ((), (), s32[]{:S(2)}) async-start(), calls=%async_computation.6 | async-start | bytes 4718592 | tf_op jit(solution)/shard_map/all_gather | solution.py:68
  40.5 5.9 %copy-start.2 = (bf16[512,1024]{1,0:T(8,128)(2,1)S(1)}, bf16[512,1024]{1,0:T(8,128)(2,1)}, u32[]{:S(2)}) copy-start(bf16[512,1024]{1,0:T(8,128)(2,1)} %param.7) | copy-start | bytes 3145732
  58.9 6.2 %copy-start.4 = (bf16[128,2,1024]{2,1,0:T(2,128)(2,1)S(1)}, bf16[128,2,1024]{2,1,0:T(2,128)(2,1)}, u32[]{:S(2)}) copy-start(bf16[128,2,1024]{2,1,0:T(2,128)(2,1)} %param.10) | copy-start | bytes 1572868
  58.9 7.3 %copy-start.5 = (s32[1,2,512]{2,1,0:T(2,128)S(1)}, s32[1,2,512]{2,1,0:T(2,128)}, u32[]{:S(2)}) copy-start(s32[1,2,512]{2,1,0:T(2,128)} %param.12) | copy-start | bytes 12292
  58.9 7.4 %copy-start.6 = (f32[1,2,512]{2,1,0:T(2,128)S(1)}, f32[1,2,512]{2,1,0:T(2,128)}, u32[]{:S(2)}) copy-start(f32[1,2,512]{2,1,0:T(2,128)} %param.13) | copy-start | bytes 12292
  58.9 81.4 %all-to-all-start.1 = ((bf16[32,48,2,1024]{3,1,2,0:T(8,128)(2,1)}), bf16[32,48,2,1024]{3,1,2,0:T(8,128)(2,1)}, u32[]{:S(2)}, u32[]{:S(2)}) async-start(bf16[32,48,2,1024]{3,1,2,0:T(8,128)(2,1)} %maximum_select_fusion), calls=%async_computation.1 | async-start | bytes 12582912 | tf_op jit(solution)/shard_map/all_to_all | solution.py:60
  65.0 139.9 %all-gather.3.cloned.1.call-start = ((), (), s32[]{:S(2)}) async-start(), calls=%async_computation.5 | async-start | bytes 4718592 | tf_op jit(solution)/shard_map/all_gather | solution.py:69
  66.0 233.8 %reduce-scatter.9.cloned.1.call-start = ((), (), s32[]{:S(2)}) async-start(), calls=%async_computation.8 | async-start | bytes 4718592
  189.1 4.7 %copy-start.3 = (f32[1024,1,1024]{2,0,1:T(8,128)S(1)}, f32[1024,1,1024]{2,0,1:T(8,128)}, u32[]{:S(2)}) copy-start(f32[1024,1,1024]{2,0,1:T(8,128)} %copy.68) | copy-start | bytes 12582916
  193.8 4.3 %copy-start.7 = (f32[2,512,1024]{2,1,0:T(8,128)}, f32[2,512,1024]{2,1,0:T(8,128)S(1)}, u32[]{:S(2)}) copy-start(f32[2,512,1024]{2,1,0:T(8,128)S(1)} %fusion.25) | copy-start | bytes 12582916
  204.6 112.6 %reduce-scatter.7.cloned.1.call-start = ((), (), s32[]{:S(2)}) async-start(), calls=%async_computation.7 | async-start | bytes 4718592
  213.2 4.4 %copy-start.8 = (bf16[2,512,1024]{2,1,0:T(8,128)(2,1)}, bf16[2,512,1024]{2,1,0:T(8,128)(2,1)S(1)}, u32[]{:S(2)}) copy-start(bf16[2,512,1024]{2,1,0:T(8,128)(2,1)S(1)} %fusion.8) | copy-start | bytes 6291460
  236.9 47.3 %all-to-all-start.2 = ((bf16[32,48,1024]{2,1,0:T(8,128)(2,1)}), bf16[32,48,1024]{2,1,0:T(8,128)(2,1)}, u32[]{:S(2)}, u32[]{:S(2)}) async-start(bf16[32,48,1024]{2,1,0:T(8,128)(2,1)} %bitcast.73), calls=%async_computation.2 | async-start | bytes 6291456 | tf_op jit(solution)/shard_map/all_to_all | solution.py:110
  284.2 35.5 %copy-start.1 = (bf16[512,1024]{1,0:T(8,128)(2,1)S(1)}, bf16[512,1024]{1,0:T(8,128)(2,1)}, u32[]{:S(2)}) copy-start(bf16[512,1024]{1,0:T(8,128)(2,1)} %param.8) | copy-start | bytes 3145732
Sparse Core Ops, SparseCore 0:
  10.4 57.7 all-gather.4
  70.6 55.2 all-gather.2
  204.7 56.1 reduce-scatter.8
  263.3 53.9 reduce-scatter.6
where the time goes:
time: 328 us; the launch traced here: 326 us
  waiting for transfers between devices  119 us (36%)
  local copies, waits for them, and re-layouts  82.6 us (25%)
  other arithmetic  47.4 us (14%)
  matrix products  35.1 us (11%)
  starting transfers between devices  14.1 us (4%)
  between operations  14.1 us (4%)
  blocking collectives  13.6 us (4%)
    all_to_all x1, waiting for transfers between devices, on_device(): lax.all_to_all(outgoing, 'expert', split_axis=0, concat_axis=0, tiled=True)  74 us
    all_to_all x1, waiting for transfers between devices, on_device(): lax.all_to_all(back_rows.reshape(n_peers, slots, width), 'expert', split_...  30.3 us
    unnamed x31, local copies, waits for them, and re-layouts  26.1 us
    gather x1, local copies, waits for them, and re-layouts, on_device(): gathered = arrived.reshape(n_peers * slots, 2, width)[safe_slot]  18.5 us
    unnamed x6, waiting for transfers between devices  15.1 us
    scatter-add x1, other arithmetic, on_device(): jax.ops.segment_sum(returned.reshape(n_peers * slots, width).astype(jnp.f...  14.5 us
    all_to_all x1, blocking collectives, on_device(): lax.all_to_all(table.reshape(n_peers, slots), 'expert', split_axis=0, con...  13.6 us
    all_to_all x1, local copies, waits for them, and re-layouts, on_device(): lax.all_to_all(outgoing, 'expert', split_axis=0, concat_axis=0, tiled=True)  12.7 us
  transfers between devices with their start and end apart: 6, of which 3 were waited for; matrix products, arithmetic and copies ran while one was open for 49% of the time, Pallas kernels for 0%

commit v1 on v0

v1 whole, which is shorter than its diff:
```python
import jax
import jax.numpy as jnp
from jax import lax
from jax.sharding import PartitionSpec as P

gelu_coef = 0.7978845608028654
cubic_coef = 0.044715
bf16 = jnp.bfloat16
f32 = jnp.float32


def gelu_parts(value):
    inner = gelu_coef * (value + cubic_coef * value * value * value)
    tangent = jnp.tanh(inner)
    result = 0.5 * value * (1.0 + tangent)
    slope = 0.5 * (1.0 + tangent) + 0.5 * value * (1.0 - tangent * tangent) * gelu_coef * (
        1.0 + 3.0 * cubic_coef * value * value
    )
    return (result, slope)


def dot(a, b, ca, cb):
    return lax.dot_general(a, b, (((ca,), (cb,)), ((), ())), preferred_element_type=f32)


def on_device(activations, out_grad, w_in, w_out, token_lists, valid_mask, gate_weights):
    n_peers = lax.axis_size("expert")
    tok_local, width = activations.shape
    _, exp_local, cap_len = token_lists.shape
    shard, _, hid = w_in.shape
    picks = exp_local * cap_len
    slots = max(2, 3 * picks // (2 * n_peers))
    n_slots = n_peers * slots

    w_in_rows = w_in.reshape(shard, exp_local * hid)
    w_out_rows = w_out.reshape(w_out.shape[0], exp_local * width)
    full_in = lax.all_gather(w_in_rows, "dp", axis=0, tiled=True)
    full_out = lax.all_gather(w_out_rows, "dp", axis=0, tiled=True)

    flat = token_lists.reshape(picks)
    live = valid_mask.reshape(picks) == 1
    owners = jnp.where(live, flat // tok_local, -1)
    local = flat % tok_local
    peers = jnp.arange(n_peers, dtype=jnp.int32)
    hits = (owners[:, None] == peers[None, :]).astype(bf16)
    order = jnp.arange(picks, dtype=jnp.int32)
    earlier = (order[None, :] < order[:, None]).astype(bf16)
    rank_all = dot(earlier, hits, 1, 0)
    before = jnp.sum(rank_all * hits.astype(f32), axis=1).astype(jnp.int32)
    slot_of = jnp.where(live, owners * slots + before, -1)
    place = (before[:, None] == jnp.arange(slots, dtype=jnp.int32)[None, :]).astype(bf16)
    high = (local // 32 + 1).astype(bf16)[:, None]
    low = (local % 32).astype(bf16)[:, None]
    both = jnp.concatenate([hits * high, hits * low], axis=1)
    coded = dot(both, place, 0, 0).astype(jnp.int32)
    table = coded[:n_peers] * 32 + coded[n_peers:] - 32

    wanted = lax.all_to_all(table, "expert", split_axis=0, concat_axis=0, tiled=True)
    wanted = wanted.reshape(n_slots)
    toks = jnp.arange(tok_local, dtype=jnp.int32)
    send = (wanted[:, None] == toks[None, :]).astype(bf16)
    out_x = dot(send, activations, 1, 0).astype(bf16)
    out_g = dot(send, out_grad, 1, 0).astype(bf16)
    got_x = lax.all_to_all(out_x, "expert", split_axis=0, concat_axis=0, tiled=True)
    got_g = lax.all_to_all(out_g, "expert", split_axis=0, concat_axis=0, tiled=True)

    pick = (slot_of[:, None] == jnp.arange(n_slots, dtype=jnp.int32)[None, :]).astype(bf16)
    picked_in = dot(pick, got_x, 1, 0).astype(bf16)
    gates = (gate_weights * valid_mask.astype(f32)).reshape(picks)

    ins, outs, grads, gate_parts = [], [], [], []
    hiddens, slopes = [], []
    for e in range(exp_local):
        rows = slice(e * cap_len, (e + 1) * cap_len)
        hidden, slope = gelu_parts(dot(picked_in[rows], full_in[:, e * hid : (e + 1) * hid], 1, 0))
        hiddens.append(hidden.astype(bf16))
        slopes.append(slope)
    picked_grad = dot(pick, got_g, 1, 0).astype(bf16)
    scaled_all = (gates[:, None] * picked_grad.astype(f32)).astype(bf16)
    pre_grads = []
    for e in range(exp_local):
        rows = slice(e * cap_len, (e + 1) * cap_len)
        outs.append(dot(hiddens[e], scaled_all[rows], 0, 0).astype(bf16))
    w_out_grad = lax.psum_scatter(
        jnp.concatenate(outs, axis=1), "dp", scatter_dimension=0, tiled=True
    )
    for e in range(exp_local):
        rows = slice(e * cap_len, (e + 1) * cap_len)
        w_o = full_out[:, e * width : (e + 1) * width]
        pre_grad = (dot(scaled_all[rows], w_o, 1, 1) * slopes[e]).astype(bf16)
        pre_grads.append(pre_grad)
        ins.append(dot(picked_in[rows], pre_grad, 0, 0).astype(bf16))
    w_in_grad = lax.psum_scatter(
        jnp.concatenate(ins, axis=1), "dp", scatter_dimension=0, tiled=True
    )
    for e in range(exp_local):
        rows = slice(e * cap_len, (e + 1) * cap_len)
        grads.append(dot(pre_grads[e], full_in[:, e * hid : (e + 1) * hid], 1, 1).astype(bf16))
        expert_out = dot(hiddens[e], full_out[:, e * width : (e + 1) * width], 1, 0)
        gate_parts.append(jnp.sum(picked_grad[rows].astype(f32) * expert_out, axis=-1))
    in_grad = jnp.concatenate(grads, axis=0)
    back = dot(pick, in_grad, 0, 0).astype(bf16)
    returned = lax.all_to_all(back, "expert", split_axis=0, concat_axis=0, tiled=True)
    token_grad = dot(send, returned, 0, 0).astype(bf16)
    return (
        token_grad,
        jnp.stack(gate_parts)[None],
        w_in_grad.reshape(shard, exp_local, hid),
        w_out_grad.reshape(w_out.shape[0], exp_local, width),
    )


def solution(mesh):
    tokens = P(("dp", "expert"), None)
    split = P("dp", "expert", None)
    return jax.shard_map(
        on_device,
        mesh=mesh,
        in_specs=(tokens, tokens, split, split, split, split, split),
        out_specs=(tokens, split, split, split),
        check_vma=False,
    )
```

time: 328 us -> 270 us (0.82)
  local copies, waits for them, and re-layouts: 82.6 us -> 26.6 us
  other arithmetic: 47.4 us -> 7.05 us
  matrix products: 35.1 us -> 59.7 us
  waiting for transfers between devices: 119 us -> 127 us
  starting transfers between devices: 14.1 us -> 20.3 us
    gather x3 -> x0, local copies, waits for them, and re-layouts: 30.2 us -> none  [the longest x1 18.5 us: on_device(): gathered = arrived.reshape(n_peers * slots, 2, width)[safe_slot]]
    dot_general x6 -> x20, matrix products: 35.1 us -> 59.7 us  [dot(): lax.dot_general(a, b, (((ca,), (cb,)), ((), ())), preferred_element_type=...]
    select_n x8 -> x1, other arithmetic: 14.6 us -> 0.01 us  [on_device(): owners = jnp.where(live, flat // tok_local, -1)]
    scatter-add x1 -> x0, other arithmetic: 14.5 us -> none  [on_device(): jax.ops.segment_sum(returned.reshape(n_peers * slots, width).astype(jnp.f...]
    all_to_all x4 -> x2, local copies, waits for them, and re-layouts: 13.4 us -> 0.58 us  [on_device(): lax.all_to_all(table, 'expert', split_axis=0, concat_axis=0, tiled=True)]
    scatter x2 -> x0, local copies, waits for them, and re-layouts: 11.8 us -> none  [the longest x1 7.48 us: on_device(): back_rows = jnp.zeros((n_peers * slots, width), jnp.bfloat16).at[slot_of]...]
    unnamed x6, waiting for transfers between devices: 15.1 us -> 25.9 us
    another operation x3 -> x0, other arithmetic: 9.14 us -> none
  transfers between devices with their start and end apart: 6 -> 7, of which waited for: 3 -> 4; matrix products, arithmetic and copies ran while one was open for 49% -> 31% of each run, Pallas kernels for 0% -> 0%
where the time goes in v1:
time: 270 us; the launch traced here: 268 us
  waiting for transfers between devices  127 us (47%)
  matrix products  59.7 us (22%)
  local copies, waits for them, and re-layouts  26.6 us (10%)
  starting transfers between devices  20.3 us (8%)
  between operations  14.1 us (5%)
  blocking collectives  13.6 us (5%)
  other arithmetic  7.05 us (3%)
    dot_general x20, matrix products, dot(): lax.dot_general(a, b, (((ca,), (cb,)), ((), ())), preferred_element_type=...  59.7 us
    all_to_all x1, waiting for transfers between devices, on_device(): lax.all_to_all(out_x, 'expert', split_axis=0, concat_axis=0, tiled=True)  35.2 us
    all_to_all x1, waiting for transfers between devices, on_device(): lax.all_to_all(back, 'expert', split_axis=0, concat_axis=0, tiled=True)  33.2 us
    all_to_all x1, waiting for transfers between devices, on_device(): lax.all_to_all(out_g, 'expert', split_axis=0, concat_axis=0, tiled=True)  32.9 us
    unnamed x6, waiting for transfers between devices  25.9 us
    unnamed x46, local copies, waits for them, and re-layouts  25.9 us
    all_to_all x1, blocking collectives, on_device(): lax.all_to_all(table, 'expert', split_axis=0, concat_axis=0, tiled=True)  13.6 us
    all_to_all x1, starting transfers between devices, on_device(): lax.all_to_all(out_g, 'expert', split_axis=0, concat_axis=0, tiled=True)  6.9 us
  transfers between devices with their start and end apart: 7, of which 4 were waited for; matrix products, arithmetic and copies ran while one was open for 31% of the time, Pallas kernels for 0%

profile of v1, /device:TPU:2, one launch (start us, length us, event | category | flops | bytes accessed | tf_op | source)
XLA Modules:
  0.0 268.5 jit_solution(2483923718885038905)
XLA Ops:
  7.2 2.0 copy.34
  11.9 13.6 %all_to_all.45 = s32[32,1,48]{2,1,0:T(1,128)S(1)} all-to-all(s32[32,1,48]{2,1,0:T(1,128)S(1)} %copy.20), channel_id=1, replica_groups=mesh['dp'=8,'expert'=32] {'expert'}, dimensions={0} | all-to-all | bytes 12288 | tf_op jit(solution)/shard_map/all_to_all | solution.py:58
  26.8 3.5 %convolution_convert_fusion = bf16[1536,1024]{1,0:T(8,128)(2,1)} fusion(bf16[512,1024]{1,0:T(8,128)(2,1)S(1)} %copy-done, s32[1536]{0:T(1024)S(1)} %eq.78), kind=kOutput, calls=%fused_computation.10 | convolution fusion | flops 1612972032 | bytes 4200448 | tf_op jit(solution)/shard_map/dot_general | solution.py:23
  30.3 6.0 %all-to-all-start.2 = ((bf16[32,48,1024]{2,1,0:T(8,128)(2,1)}), bf16[32,48,1024]{2,1,0:T(8,128)(2,1)}, u32[]{:S(2)}, u32[]{:S(2)}) async-start(bf16[32,48,1024]{2,1,0:T(8,128)(2,1)} %bitcast.36), calls=%async_computation.2 | async-start | bytes 6291456 | tf_op jit(solution)/shard_map/all_to_all | solution.py:64
  37.3 3.6 %convolution_convert_fusion.1 = bf16[1536,1024]{1,0:T(8,128)(2,1)} fusion(bf16[512,1024]{1,0:T(8,128)(2,1)S(1)} %copy-done.9, s32[1536]{0:T(1024)S(1)} %eq.78), kind=kOutput, calls=%fused_computation.11 | convolution fusion | flops 1612972032 | bytes 4200448 | tf_op jit(solution)/shard_map/dot_general | solution.py:23
  40.9 35.2 %all-to-all-done.2 = bf16[32,48,1024]{2,1,0:T(8,128)(2,1)} async-done(((bf16[32,48,1024]{2,1,0:T(8,128)(2,1)}), bf16[32,48,1024]{2,1,0:T(8,128)(2,1)}, u32[]{:S(2)}, u32[]{:S(2)}) %all-to-all-start.2) | async-done | bytes 3145760 | tf_op jit(solution)/shard_map/all_to_all | solution.py:64
  76.1 6.9 %all-to-all-start.1 = ((bf16[32,48,1024]{2,1,0:T(8,128)(2,1)}), bf16[32,48,1024]{2,1,0:T(8,128)(2,1)}, u32[]{:S(2)}, u32[]{:S(2)}) async-start(bf16[32,48,1024]{2,1,0:T(8,128)(2,1)} %bitcast.34), calls=%async_computation.1 | async-start | bytes 6291456 | tf_op jit(solution)/shard_map/all_to_all | solution.py:65
  83.3 6.7 %fusion.27 = bf16[1024,1024]{1,0:T(8,128)(2,1)} fusion(bf16[1536,1024]{1,0:T(8,128)(2,1)} %bitcast.4, s32[1024]{0:T(1024)S(1)} %get-tuple-element.19), kind=kOutput, calls=%fused_computation.43 | convolution fusion | flops 3223846912 | bytes 5246976 | tf_op jit(solution)/shard_map/dot_general | solution.py:23
  90.0 32.9 %all-to-all-done.1 = bf16[32,48,1024]{2,1,0:T(8,128)(2,1)} async-done(((bf16[32,48,1024]{2,1,0:T(8,128)(2,1)}), bf16[32,48,1024]{2,1,0:T(8,128)(2,1)}, u32[]{:S(2)}, u32[]{:S(2)}) %all-to-all-start.1) | async-done | bytes 3145760 | tf_op jit(solution)/shard_map/all_to_all | solution.py:65
  122.9 7.5 %multiply_convert_fusion = (bf16[1024,1024]{0,1:T(8,128)(2,1)}, bf16[1024,1024]{0,1:T(8,128)(2,1)}) fusion(f32[1024]{0:T(1024)S(1)} %bitcast.46, bf16[1536,1024]{1,0:T(8,128)(2,1)} %bitcast.2, s32[1024]{0:T(1024)S(1)} %get-tuple-element.19), kind=kOutput, calls=%fused_computation.6 | convolution fusion | flops 3226992640 | bytes 7348224 | tf_op jit(solution)/shard_map/dot_general | solution.py:23
  130.3 3.3 %fusion.30 = f32[512,1024]{1,0:T(8,128)S(1)} fusion(bf16[1024,2048]{1,0:T(8,128)(2,1)} %all-gather.5.cloned.1.call-done, bf16[1024,1024]{1,0:T(8,128)(2,1)} %fusion.27), kind=kOutput, calls=%fused_computation.50 | convolution fusion | flops 1073741824 | bytes 5242880 | tf_op jit(solution)/shard_map/dot_general | solution.py:23
  135.7 1.4 convolution_convert_fusion.3
  137.2 1.4 convolution_convert_fusion.2
  138.6 2.5 pad_maximum_fusion.1
  141.0 6.5 %copy.29 = bf16[1024,2048]{1,0:T(8,128)(2,1)} copy(bf16[1024,2048]{0,1:T(8,128)(2,1)} %pad_maximum_fusion.1) | data formatting | bytes 8388608
  147.8 4.4 %fusion.22 = bf16[512,1024]{1,0:T(8,128)(2,1)S(1)} fusion(f32[512,1024]{1,0:T(8,128)S(1)} %fusion.30, bf16[1024,2048]{1,0:T(8,128)(2,1)} %all-gather.3.cloned.1.call-done, bf16[1024,1024]{0,1:T(8,128)(2,1)} %get-tuple-element.21), kind=kOutput, calls=%fused_computation.34 | convolution fusion | flops 1083703296 | bytes 6291456 | tf_op jit(solution)/shard_map/dot_general | solution.py:23
  152.3 1.3 convolution_convert_fusion.4
  155.7 2.4 fusion.15
  159.1 1.3 convolution_convert_fusion.5
  160.4 2.5 pad_maximum_fusion
  162.9 6.5 %copy.27 = bf16[1024,2048]{1,0:T(8,128)(2,1)} copy(bf16[1024,2048]{0,1:T(8,128)(2,1)} %pad_maximum_fusion) | data formatting | bytes 8388608
  169.4 3.4 %fusion.47 = bf16[512,1024]{1,0:T(8,128)(2,1)S(1)} fusion(bf16[512,1024]{1,0:T(8,128)(2,1)} %copy-done.16, bf16[1024,2048]{1,0:T(8,128)(2,1)} %all-gather.5.cloned.1.call-done), kind=kOutput, calls=%fused_computation.67 | convolution fusion | flops 1074266112 | bytes 4194304 | tf_op jit(solution)/shard_map/dot_general | solution.py:23
  172.8 1.3 fusion.50
  174.1 5.5 %fusion.4 = bf16[1536,1024]{1,0:T(8,128)(2,1)} fusion(s32[1024]{0:T(1024)S(1)} %get-tuple-element.19, bf16[512,1024]{1,0:T(8,128)(2,1)S(1)} %fusion.50, bf16[512,1024]{1,0:T(8,128)(2,1)S(1)} %fusion.47), kind=kOutput, calls=%fused_computation.9 | convolution fusion | flops 3228565504 | bytes 5246976 | tf_op jit(solution)/shard_map/dot_general | solution.py:23
  179.7 6.8 %all-to-all-start.3 = ((bf16[32,48,1024]{2,1,0:T(8,128)(2,1)}), bf16[32,48,1024]{2,1,0:T(8,128)(2,1)}, u32[]{:S(2)}, u32[]{:S(2)}) async-start(bf16[32,48,1024]{2,1,0:T(8,128)(2,1)} %bitcast.35), calls=%async_computation.3 | async-start | bytes 6291456 | tf_op jit(solution)/shard_map/all_to_all | solution.py:103
  186.5 4.1 %multiply_reduce_fusion.1 = f32[512]{0:T(512)S(1)} fusion(bf16[1024,2048]{1,0:T(8,128)(2,1)} %all-gather.3.cloned.1.call-done, bf16[1024,1024]{0,1:T(8,128)(2,1)} %get-tuple-element.22, f32[512,1024]{1,0:T(8,128)} %copy-done.10), kind=kOutput, calls=%fused_computation.40 | convolution fusion | flops 1080032768 | bytes 5244928 | tf_op jit(solution)/shard_map/dot_general | solution.py:23
  191.1 1.4 multiply_reduce_fusion
  193.1 33.2 %all-to-all-done.3 = bf16[32,48,1024]{2,1,0:T(8,128)(2,1)} async-done(((bf16[32,48,1024]{2,1,0:T(8,128)(2,1)}), bf16[32,48,1024]{2,1,0:T(8,128)(2,1)}, u32[]{:S(2)}, u32[]{:S(2)}) %all-to-all-start.3) | async-done | bytes 3145760 | tf_op jit(solution)/shard_map/all_to_all | solution.py:103
  226.3 4.9 %fusion.53 = bf16[512,1024]{1,0:T(8,128)(2,1)} fusion(bf16[1536,1024]{1,0:T(8,128)(2,1)} %bitcast.6, s32[1536]{0:T(1024)S(1)} %eq.78), kind=kOutput, calls=%fused_computation.69 | convolution fusion | flops 1611923456 | bytes 4200448 | tf_op jit(solution)/shard_map/dot_general | solution.py:23
  231.2 1.3 copy.30
  233.6 25.9 %reduce-scatter.7.cloned.1.call-done = bf16[128,2048]{1,0:T(8,128)(2,1)} async-done(((bf16[1024,2048]{1,0:T(8,128)(2,1)}), bf16[128,2048]{1,0:T(8,128)(2,1)}) %reduce-scatter.7.cloned.1.call-update) | async-done | bytes 524304
  259.5 1.3 copy.28
  (68 shorter events, 13.9 us)
Async XLA Ops:
  7.2 19.6 %copy-start = (bf16[512,1024]{1,0:T(8,128)(2,1)S(1)}, bf16[512,1024]{1,0:T(8,128)(2,1)}, u32[]{:S(2)}) copy-start(bf16[512,1024]{1,0:T(8,128)(2,1)} %param.7) | copy-start | bytes 3145732
  7.2 123.2 %all-gather.5.cloned.1.call-start = ((), (), s32[]{:S(2)}) async-start(), calls=%async_computation.7 | async-start | bytes 4718592 | tf_op jit(solution)/shard_map/all_gather | solution.py:37
  30.3 6.0 %copy-start.2 = (bf16[128,2,1024]{2,1,0:T(2,128)(2,1)S(1)}, bf16[128,2,1024]{2,1,0:T(2,128)(2,1)}, u32[]{:S(2)}) copy-start(bf16[128,2,1024]{2,1,0:T(2,128)(2,1)} %param.10) | copy-start | bytes 1572868
  30.3 7.0 %copy-start.9 = (bf16[512,1024]{1,0:T(8,128)(2,1)S(1)}, bf16[512,1024]{1,0:T(8,128)(2,1)}, u32[]{:S(2)}) copy-start(bf16[512,1024]{1,0:T(8,128)(2,1)} %param.8) | copy-start | bytes 3145732
  30.3 45.8 %all-to-all-start.2 = ((bf16[32,48,1024]{2,1,0:T(8,128)(2,1)}), bf16[32,48,1024]{2,1,0:T(8,128)(2,1)}, u32[]{:S(2)}, u32[]{:S(2)}) async-start(bf16[32,48,1024]{2,1,0:T(8,128)(2,1)} %bitcast.36), calls=%async_computation.2 | async-start | bytes 6291456 | tf_op jit(solution)/shard_map/all_to_all | solution.py:64
  36.3 111.5 %all-gather.3.cloned.1.call-start = ((), (), s32[]{:S(2)}) async-start(), calls=%async_computation.6 | async-start | bytes 4718592 | tf_op jit(solution)/shard_map/all_gather | solution.py:38
  76.1 7.1 %copy-start.3 = (s32[1,2,512]{2,1,0:T(2,128)S(1)}, s32[1,2,512]{2,1,0:T(2,128)}, u32[]{:S(2)}) copy-start(s32[1,2,512]{2,1,0:T(2,128)} %param.12) | copy-start | bytes 12292
  76.1 7.2 %copy-start.4 = (f32[1,2,512]{2,1,0:T(2,128)S(1)}, f32[1,2,512]{2,1,0:T(2,128)}, u32[]{:S(2)}) copy-start(f32[1,2,512]{2,1,0:T(2,128)} %param.13) | copy-start | bytes 12292
  76.1 46.7 %all-to-all-start.1 = ((bf16[32,48,1024]{2,1,0:T(8,128)(2,1)}), bf16[32,48,1024]{2,1,0:T(8,128)(2,1)}, u32[]{:S(2)}, u32[]{:S(2)}) async-start(bf16[32,48,1024]{2,1,0:T(8,128)(2,1)} %bitcast.34), calls=%async_computation.1 | async-start | bytes 6291456 | tf_op jit(solution)/shard_map/all_to_all | solution.py:65
  83.0 148.2 %reduce-scatter.9.cloned.1.call-start = ((), (), s32[]{:S(2)}) async-start(), calls=%async_computation.9 | async-start | bytes 4718592
  130.3 3.3 %copy-start.5 = (bf16[1024,2048]{1,0:T(8,128)(2,1)S(1)}, bf16[1024,2048]{1,0:T(8,128)(2,1)}, u32[]{:S(2)}) copy-start(bf16[1024,2048]{1,0:T(8,128)(2,1)} %all-gather.5.cloned.1.call-done) | copy-start | bytes 12582916
  130.3 3.8 %copy-start.12 = (bf16[1024,1024]{1,0:T(8,128)(2,1)S(1)}, bf16[1024,1024]{1,0:T(8,128)(2,1)}, u32[]{:S(2)}) copy-start(bf16[1024,1024]{1,0:T(8,128)(2,1)} %fusion.27) | copy-start | bytes 6291460
  134.2 1.6 copy-start.14
  135.4 1.7 copy-start.10
  147.5 112.0 %reduce-scatter.7.cloned.1.call-start = ((), (), s32[]{:S(2)}) async-start(), calls=%async_computation.8 | async-start | bytes 4718592
  147.8 4.4 %copy-start.13 = (bf16[1024,1024]{1,0:T(8,128)(2,1)S(1)}, bf16[1024,1024]{1,0:T(8,128)(2,1)}, u32[]{:S(2)}) copy-start(bf16[1024,1024]{1,0:T(8,128)(2,1)} %fusion.27) | copy-start | bytes 6291460
  152.2 2.2 copy-start.7
  152.2 2.9 %copy-start.11 = (f32[512,1024]{1,0:T(8,128)S(1)}, f32[512,1024]{1,0:T(8,128)}, u32[]{:S(2)}) copy-start(f32[512,1024]{1,0:T(8,128)} %copy-done.10) | copy-start | bytes 6291460
  152.3 3.5 %copy-start.15 = (bf16[1024,1024]{0,1:T(8,128)(2,1)S(1)}, bf16[1024,1024]{0,1:T(8,128)(2,1)}, u32[]{:S(2)}) copy-start(bf16[1024,1024]{0,1:T(8,128)(2,1)} %get-tuple-element.21) | copy-start | bytes 6291460
  158.2 1.0 copy-start.16
  169.4 3.4 %copy-start.6 = (bf16[1024,2048]{1,0:T(8,128)(2,1)S(1)}, bf16[1024,2048]{1,0:T(8,128)(2,1)}, u32[]{:S(2)}) copy-start(bf16[1024,2048]{1,0:T(8,128)(2,1)} %all-gather.5.cloned.1.call-done) | copy-start | bytes 12582916
  179.7 46.6 %all-to-all-start.3 = ((bf16[32,48,1024]{2,1,0:T(8,128)(2,1)}), bf16[32,48,1024]{2,1,0:T(8,128)(2,1)}, u32[]{:S(2)}, u32[]{:S(2)}) async-start(bf16[32,48,1024]{2,1,0:T(8,128)(2,1)} %bitcast.35), calls=%async_computation.3 | async-start | bytes 6291456 | tf_op jit(solution)/shard_map/all_to_all | solution.py:103
  186.5 4.1 %copy-start.8 = (bf16[1024,2048]{1,0:T(8,128)(2,1)S(1)}, bf16[1024,2048]{1,0:T(8,128)(2,1)}, u32[]{:S(2)}) copy-start(bf16[1024,2048]{1,0:T(8,128)(2,1)} %all-gather.3.cloned.1.call-done) | copy-start | bytes 12582916
  186.5 4.6 %copy-start.17 = (bf16[1024,1024]{0,1:T(8,128)(2,1)S(1)}, bf16[1024,1024]{0,1:T(8,128)(2,1)}, u32[]{:S(2)}) copy-start(bf16[1024,1024]{0,1:T(8,128)(2,1)} %get-tuple-element.22) | copy-start | bytes 6291460
  226.3 35.7 %copy-start.1 = (bf16[512,1024]{1,0:T(8,128)(2,1)S(1)}, bf16[512,1024]{1,0:T(8,128)(2,1)}, u32[]{:S(2)}) copy-start(bf16[512,1024]{1,0:T(8,128)(2,1)} %param.7) | copy-start | bytes 3145732
Sparse Core Ops, SparseCore 0:
  10.4 57.7 all-gather.4
  70.5 53.4 all-gather.2
  147.7 55.4 reduce-scatter.8
  205.5 53.9 reduce-scatter.6

commit v2 on v1

v2 whole, which is shorter than its diff:
```python
import functools
import jax
import jax.numpy as jnp
from jax import lax
from jax.experimental import pallas as pl
from jax.experimental.pallas import tpu as pltpu
from jax.sharding import PartitionSpec as P

gelu_coef = 0.7978845608028654
cubic_coef = 0.044715
bf16 = jnp.bfloat16
f32 = jnp.float32
i32 = jnp.int32
VMEM_BYTES = 67043328


def gelu_parts(value):
    inner = gelu_coef * (value + cubic_coef * value * value * value)
    tangent = jnp.tanh(inner)
    result = 0.5 * value * (1.0 + tangent)
    slope = 0.5 * (1.0 + tangent) + 0.5 * value * (1.0 - tangent * tangent) * gelu_coef * (
        1.0 + 3.0 * cubic_coef * value * value
    )
    return (result, slope)


def dot(a, b, ca, cb):
    return lax.dot_general(a, b, (((ca,), (cb,)), ((), ())), preferred_element_type=f32)


def loop(count, body):
    def step(i, carry):
        body(i)
        return carry

    lax.fori_loop(0, count, step, 0)


def layer_kernel(
    n_peers, n_ring, slots, group, tile,
    x_ref, g_ref, wi_ref, wo_ref, table_ref, slot_col, slot_row, gate_col,
    tok_ref, gate_ref, wig_ref, wog_ref,
    full, send_x, send_g, recv_x, recv_g, recv_b, sel, want,
    picked_x, picked_g, scaled, hidden, slope, pre_grad, in_grad, ring,
    ag_send, ag_recv, rs_send, rs_recv, t_send, t_recv, a_send, a_recv, own_sem,
):
    me = lax.axis_index("expert")
    z = lax.axis_index("dp")
    tokens, width = x_ref.shape
    shard = wi_ref.shape[1]
    picks = slot_col.shape[0]
    cap = picks // 2
    n_slots = n_peers * slots
    span = group * slots
    half = n_ring // 2
    tiles = picks // tile
    per_expert = cap // tile

    def rows_of(i):
        return pl.ds(pl.multiple_of(i * tile, tile), tile)

    def expert_rows(e):
        return pl.ds(pl.multiple_of(e * cap, cap), cap)

    def peer_rows(p):
        return pl.ds(pl.multiple_of(p * slots, slots), slots)

    def shard_rows(s):
        return pl.ds(pl.multiple_of(s * shard, shard), shard)

    barrier = pltpu.get_barrier_semaphore()

    def greet(i):
        pl.semaphore_signal(
            barrier, inc=1, device_id={"expert": lax.rem(me + i + 1, n_peers)},
            device_id_type=pl.DeviceIdType.MESH,
        )

    loop(n_peers - 1, greet)
    for step in (1, n_ring - 1):
        pl.semaphore_signal(
            barrier, inc=1, device_id={"dp": lax.rem(z + step, n_ring)},
            device_id_type=pl.DeviceIdType.MESH,
        )
    pl.semaphore_wait(barrier, n_peers + 1)

    def neighbour(d):
        return lax.rem(z + 1 + d * (n_ring - 2), n_ring)

    def ag_copy(m, e, d, s, own):
        holder = lax.rem(z + n_ring - s + d * (2 * s), n_ring)
        place = full.at[m, e, shard_rows(holder), :]
        source = (wi_ref, wo_ref)[m].at[e] if own else place
        return pltpu.make_async_remote_copy(
            src_ref=source, dst_ref=place,
            send_sem=ag_send.at[m, e, d, s], recv_sem=ag_recv.at[m, e, d, s],
            device_id={"dp": neighbour(d)}, device_id_type=pl.DeviceIdType.MESH,
        )

    def ag_step(m, s):
        def one(j):
            e, d = j // 2, j % 2
            if s > 0:
                ag_copy(m, e, d, s - 1, False).wait_recv()
            if s < half:
                ag_copy(m, e, d, s, s == 0).start()

        def last(j):
            if s > 0:
                ag_copy(m, j, j, s - 1, False).wait_recv()
            if s < half:
                ag_copy(m, j, j, s, s == 0).start()

        def tail(e):
            ag_copy(m, e, 1 - e, s - 1, False).wait_recv()

        if s < half - 1:
            loop(4, one)
        else:
            loop(2, last)
            if s == half - 1 and s > 0:
                loop(2, tail)

    def own_copy(m, e):
        return pltpu.make_async_copy(
            (wi_ref, wo_ref)[m].at[e], full.at[m, e, shard_rows(z), :], own_sem.at[m, e]
        )

    ag_step(0, 0)
    ag_step(1, 0)

    def table_copy(q):
        return pltpu.make_async_remote_copy(
            src_ref=table_ref.at[q], dst_ref=want.at[me],
            send_sem=t_send.at[q], recv_sem=t_recv.at[me],
            device_id={"expert": q}, device_id_type=pl.DeviceIdType.MESH,
        )

    def table_arrival(p):
        return pltpu.make_async_remote_copy(
            src_ref=table_ref.at[p], dst_ref=want.at[p],
            send_sem=t_send.at[p], recv_sem=t_recv.at[p],
            device_id={"expert": p}, device_id_type=pl.DeviceIdType.MESH,
        )

    def other(i):
        return lax.rem(me + lax.rem((i + 1) * 13, n_peers), n_peers)

    loop(n_peers - 1, lambda i: table_copy(other(i)).start())
    for m in range(2):
        for e in range(2):
            own_copy(m, e).start()
    mine = pltpu.make_async_copy(table_ref.at[me], want.at[me], own_sem.at[2, 0])
    mine.start()
    mine.wait()
    loop(n_peers - 1, lambda i: table_arrival(other(i)).wait_recv())

    for k in range(n_peers // group):
        asked = jnp.sum(want[k * group : (k + 1) * group], axis=0)
        token = lax.broadcasted_iota(i32, (tokens, span), 0) + 1
        sel[:, k * span : (k + 1) * span] = jnp.where(token == asked, 1.0, 0.0).astype(bf16)

    def gather(source, target):
        for k in range(n_peers // group):
            rows = slice(k * span, (k + 1) * span)
            target[rows, :] = dot(sel[:, rows], source[...], 0, 0).astype(bf16)

    def row_copy(phase, source, target, q):
        return pltpu.make_async_remote_copy(
            src_ref=source.at[peer_rows(q), :], dst_ref=target.at[peer_rows(me), :],
            send_sem=a_send.at[phase, q], recv_sem=a_recv.at[phase, me],
            device_id={"expert": q}, device_id_type=pl.DeviceIdType.MESH,
        )

    def row_arrival(phase, source, target, p):
        return pltpu.make_async_remote_copy(
            src_ref=source.at[peer_rows(p), :], dst_ref=target.at[peer_rows(p), :],
            send_sem=a_send.at[phase, p], recv_sem=a_recv.at[phase, p],
            device_id={"expert": p}, device_id_type=pl.DeviceIdType.MESH,
        )

    def own_rows(phase, source, target):
        return pltpu.make_async_copy(
            source.at[peer_rows(me), :], target.at[peer_rows(me), :], own_sem.at[3, phase]
        )

    def send_all(phase, source, target):
        loop(n_peers - 1, lambda i: row_copy(phase, source, target, other(i)).start())
        own_rows(phase, source, target).start()

    def receive_all(phase, source, target):
        own_rows(phase, source, target).wait()
        loop(n_peers - 1, lambda i: row_arrival(phase, source, target, other(i)).wait_recv())

    def sent_all(phase, source, target):
        loop(n_peers - 1, lambda i: row_copy(phase, source, target, other(i)).wait_send())

    gather(x_ref, send_x)
    send_all(0, send_x, recv_x)
    if half > 1:
        ag_step(0, 1)
    gather(g_ref, send_g)
    send_all(1, send_g, recv_g)
    for s in range(2, half):
        ag_step(0, s)
    if half > 1:
        ag_step(1, 1)
    ag_step(0, half)
    for e in range(2):
        own_copy(0, e).wait()
    receive_all(0, send_x, recv_x)

    def pick_tile(i):
        at = lax.broadcasted_iota(i32, (tile, n_slots), 1)
        return jnp.where(slot_col[rows_of(i), :] == at, 1.0, 0.0).astype(bf16)

    def forward(i):
        rows = rows_of(i)
        picked = dot(pick_tile(i), recv_x[...], 1, 0).astype(bf16)
        picked_x[rows, :] = picked
        value, grade = gelu_parts(dot(picked, full[0, i // per_expert], 1, 0))
        hidden[rows, :] = value.astype(bf16)
        slope[rows, :] = grade

    loop(tiles, forward)
    for s in range(2, half + 1):
        ag_step(1, s)
    if half == 1:
        ag_step(1, 1)
    for e in range(2):
        own_copy(1, e).wait()
    receive_all(1, send_g, recv_g)

    def arrive_grad(i):
        rows = rows_of(i)
        grad = dot(pick_tile(i), recv_g[...], 1, 0).astype(bf16)
        picked_g[rows, :] = grad
        scaled[rows, :] = (gate_col[rows, :] * grad.astype(f32)).astype(bf16)

    loop(tiles, arrive_grad)

    def part(m, e, t):
        columns = pl.ds(pl.multiple_of(t * shard, shard), shard)
        left, right = ((picked_x, pre_grad), (hidden, scaled))[m]
        return dot(left[expert_rows(e), columns], right[expert_rows(e), :], 0, 0)

    def rs_copy(m, e, d, s):
        return pltpu.make_async_remote_copy(
            src_ref=ring.at[m, e, d, s], dst_ref=ring.at[m, e, d, s + 1],
            send_sem=rs_send.at[m, e, d, s], recv_sem=rs_recv.at[m, e, d, s],
            device_id={"dp": neighbour(d)}, device_id_type=pl.DeviceIdType.MESH,
        )

    def rs_hop(m, e, d, s, hops):
        far = hops - s
        block = part(m, e, lax.rem(z + n_ring + far - 2 * d * far, n_ring))
        if s > 0:
            rs_copy(m, e, d, s - 1).wait_recv()
            block = block + ring[m, e, d, s].astype(f32)
        ring[m, e, d, s] = block.astype(bf16)
        rs_copy(m, e, d, s).start()

    def rs_step(m, s):
        loop(2, lambda e: rs_hop(m, e, e, s, half))
        if s < half - 1:
            loop(2, lambda e: rs_hop(m, e, 1 - e, s, half - 1))

    def rs_final(m, target):
        def one(e):
            total = part(m, e, z)
            rs_copy(m, e, e, half - 1).wait_recv()
            total = total + ring[m, e, e, half].astype(f32)
            if half > 1:
                rs_copy(m, e, 1 - e, half - 2).wait_recv()
                total = total + ring[m, e, 1 - e, half - 1].astype(f32)
            target[e] = total.astype(bf16)

        loop(2, one)

    def backward(i):
        rows = rows_of(i)
        wide = dot(scaled[rows, :], full[1, i // per_expert], 1, 1)
        pre_grad[rows, :] = (wide * slope[rows, :]).astype(bf16)

    def to_input(i):
        rows = rows_of(i)
        in_grad[rows, :] = dot(pre_grad[rows, :], full[0, i // per_expert], 1, 1).astype(bf16)

    def back(k):
        at = lax.broadcasted_iota(i32, (span, picks), 0) + k * span
        place = jnp.where(slot_row[...] == at, 1.0, 0.0).astype(bf16)
        rows = pl.ds(pl.multiple_of(k * span, span), span)
        send_x[rows, :] = dot(place, in_grad[...], 1, 0).astype(bf16)

    def gate_part(i):
        rows = rows_of(i)
        wide = dot(hidden[rows, :], full[1, i // per_expert], 1, 0)
        gate_ref[rows, :] = jnp.sum(picked_g[rows, :].astype(f32) * wide, axis=1, keepdims=True)

    rs_step(1, 0)
    loop(tiles, backward)
    rs_step(0, 0)
    loop(tiles, to_input)
    sent_all(0, send_x, recv_x)
    loop(n_peers // group, back)
    send_all(2, send_x, recv_b)
    if half > 1:
        rs_step(1, 1)
        rs_step(0, 1)
    loop(tiles, gate_part)
    for s in range(2, half):
        rs_step(1, s)
        rs_step(0, s)
    receive_all(2, send_x, recv_b)
    tok_ref[...] = dot(sel[...], recv_b[...], 1, 0).astype(bf16)
    rs_final(1, wog_ref)
    rs_final(0, wig_ref)

    loop(n_peers - 1, lambda i: table_copy(other(i)).wait_send())
    sent_all(1, send_g, recv_g)
    sent_all(2, send_x, recv_b)
    for m in range(2):
        for s in range(half):
            for e in range(2):
                for d in range(2):
                    if s < half - 1 or e == d:
                        ag_copy(m, e, d, s, s == 0).wait_send()
                        rs_copy(m, e, d, s).wait_send()


def on_device(activations, out_grad, w_in, w_out, token_lists, valid_mask, gate_weights):
    n_peers = lax.axis_size("expert")
    n_ring = lax.axis_size("dp")
    me = lax.axis_index("expert")
    tok_local, width = activations.shape
    _, exp_local, cap_len = token_lists.shape
    shard, _, hid = w_in.shape
    picks = exp_local * cap_len
    slots = max(2, 3 * picks // (2 * n_peers))
    n_slots = n_peers * slots
    group = min(8, n_peers)
    tile = min(256, cap_len)

    flat = token_lists.reshape(picks)
    live = valid_mask.reshape(picks) == 1
    owners = jnp.where(live, flat // tok_local, -1)
    local = flat % tok_local
    peers = jnp.arange(n_peers, dtype=i32)
    hits = (owners[:, None] == peers[None, :]).astype(bf16)
    order = jnp.arange(picks, dtype=i32)
    earlier = (order[None, :] < order[:, None]).astype(bf16)
    rank_all = dot(earlier, hits, 1, 0)
    before = jnp.sum(rank_all * hits.astype(f32), axis=1).astype(i32)
    slot_of = jnp.where(live, owners * slots + before, -1)
    lane = before + (me % group) * slots
    place = (lane[:, None] == jnp.arange(group * slots, dtype=i32)[None, :]).astype(bf16)
    high = (local // 32).astype(bf16)[:, None]
    low = (local % 32 + 1).astype(bf16)[:, None]
    both = jnp.concatenate([hits * high, hits * low], axis=1)
    coded = dot(both, place, 0, 0).astype(i32)
    table = coded[:n_peers] * 32 + coded[n_peers:]
    gates = (gate_weights * valid_mask.astype(f32)).reshape(picks, 1)

    vmem = pl.BlockSpec(memory_space=pltpu.VMEM)
    dma = pltpu.SemaphoreType.DMA
    rows = (n_slots, width)
    half = n_ring // 2
    token_grad, gate_grad, w_in_grad, w_out_grad = pl.pallas_call(
        functools.partial(layer_kernel, n_peers, n_ring, slots, group, tile),
        out_shape=(
            jax.ShapeDtypeStruct((tok_local, width), bf16),
            jax.ShapeDtypeStruct((picks, 1), f32),
            jax.ShapeDtypeStruct((exp_local, shard, hid), bf16),
            jax.ShapeDtypeStruct((exp_local, shard, width), bf16),
        ),
        in_specs=[vmem] * 8,
        out_specs=(vmem,) * 4,
        scratch_shapes=[
            pltpu.VMEM((2, exp_local, width, hid), bf16),
            pltpu.VMEM(rows, bf16),
            pltpu.VMEM(rows, bf16),
            pltpu.VMEM(rows, bf16),
            pltpu.VMEM(rows, bf16),
            pltpu.VMEM(rows, bf16),
            pltpu.VMEM((tok_local, n_slots), bf16),
            pltpu.VMEM((n_peers, 1, group * slots), i32),
            pltpu.VMEM((picks, width), bf16),
            pltpu.VMEM((picks, width), bf16),
            pltpu.VMEM((picks, width), bf16),
            pltpu.VMEM((picks, hid), bf16),
            pltpu.VMEM((picks, hid), f32),
            pltpu.VMEM((picks, hid), bf16),
            pltpu.VMEM((picks, width), bf16),
            pltpu.VMEM((2, exp_local, 2, half + 1, shard, width), bf16),
            dma((2, 2, 2, half)),
            dma((2, 2, 2, half)),
            dma((2, 2, 2, half)),
            dma((2, 2, 2, half)),
            dma((n_peers,)),
            dma((n_peers,)),
            dma((3, n_peers)),
            dma((3, n_peers)),
            dma((4, 3)),
        ],
        compiler_params=pltpu.CompilerParams(
            collective_id=0, has_side_effects=True, vmem_limit_bytes=VMEM_BYTES
        ),
    )(
        activations,
        out_grad,
        w_in.transpose(1, 0, 2),
        w_out.transpose(1, 0, 2),
        table.reshape(n_peers, 1, group * slots),
        slot_of.reshape(picks, 1),
        slot_of.reshape(1, picks),
        gates,
    )
    return (
        token_grad,
        gate_grad.reshape(1, exp_local, cap_len),
        w_in_grad.transpose(1, 0, 2),
        w_out_grad.transpose(1, 0, 2),
    )


def solution(mesh):
    tokens = P(("dp", "expert"), None)
    split = P("dp", "expert", None)
    return jax.shard_map(
        on_device,
        mesh=mesh,
        in_specs=(tokens, tokens, split, split, split, split, split),
        out_specs=(tokens, split, split, split),
        check_vma=False,
    )
```

time: 270 us -> 203 us (0.75)
  Pallas kernels: 0 us -> 185 us
  waiting for transfers between devices: 127 us -> 0 us
  matrix products: 59.7 us -> 0.99 us
  starting transfers between devices: 20.3 us -> 0 us
  local copies, waits for them, and re-layouts: 26.6 us -> 10.5 us
  blocking collectives: 13.6 us -> 0 us
  between operations: 14.1 us -> 0.74 us
    pallas_call x0 -> x1, Pallas kernels: none -> 185 us  [on_device(): pl.pallas_call(functools.partial(layer_kernel, n_peers, n_ring, slots, gr...]
    all_to_all x3 -> x0, waiting for transfers between devices: 101 us -> none  [the longest x1 35.2 us: on_device(): lax.all_to_all(out_x, 'expert', split_axis=0, concat_axis=0, tiled=True)]
    dot_general x20 -> x2, matrix products: 59.7 us -> 0.99 us  [dot(): lax.dot_general(a, b, (((ca,), (cb,)), ((), ())), preferred_element_type=...]
    unnamed x6 -> x0, waiting for transfers between devices: 25.9 us -> none
    all_to_all x3 -> x0, starting transfers between devices: 19.7 us -> none  [the longest x1 6.9 us: on_device(): lax.all_to_all(out_g, 'expert', split_axis=0, concat_axis=0, tiled=True)]
    unnamed x46 -> x18, local copies, waits for them, and re-layouts: 25.9 us -> 7.72 us
    all_to_all x1 -> x0, blocking collectives: 13.6 us -> none  [on_device(): lax.all_to_all(table, 'expert', split_axis=0, concat_axis=0, tiled=True)]
    concatenate x2 -> x0, other arithmetic: 4.92 us -> none  [the longest x1 2.46 us: on_device(): jnp.concatenate(outs, axis=1)]
  transfers between devices with their start and end apart: 7 -> 0, of which waited for: 4 -> 0; matrix products, arithmetic and copies ran while one was open for 31% -> 0% of each run, Pallas kernels for 0% -> 0%
where the time goes in v2:
time: 203 us
  Pallas kernels  185 us (91%)
  local copies, waits for them, and re-layouts  10.5 us (5%)
  other arithmetic  5.28 us (3%)
    pallas_call x1, Pallas kernels, on_device(): pl.pallas_call(functools.partial(layer_kernel, n_peers, n_ring, slots, gr...  185 us
    unnamed x18, local copies, waits for them, and re-layouts  7.72 us

profile of v2, /device:TPU:2, one launch (start us, length us, event | category | flops | bytes accessed | tf_op | source)
XLA Modules:
  0.0 202.9 jit_solution(14748043079246459557)
XLA Ops:
  0.6 0.7 fusion.29
  1.3 0.7 broadcast_compare_fusion
  2.1 0.7 multiply_bitcast_fusion
  2.8 0.7 copy.30
  3.5 0.7 copy.27
  4.2 0.5 fusion.4
  4.8 0.6 add_select_fusion.5.slot_row
  5.4 0.5 fusion.3
  5.9 0.6 reshape.306.table_ref
  6.5 0.3 copy.29
  6.8 0.2 copy.31
  7.1 1.0 copy.35
  8.1 0.0 copy-start.2
  8.1 0.0 copy-start.3
  8.1 0.2 copy.22
  8.3 1.2 fusion.10.slot_col
  9.5 0.0 copy-done.2
  9.5 0.0 copy-done.3
  9.5 1.2 copy_bitcast_fusion
  10.8 185.5 %shard_map.102 = (bf16[512,1024]{1,0:T(8,128)(2,1)}, f32[1024,1]{1,0:T(8,128)}, bf16[2,128,1024]{2,1,0:T(8,128)(2,1)}, bf16[2,128,1024]{2,1,0:T(8,128)(2,1)}) custom-call(bf16[512,1024]{1,0:T(8,128)(2,1)} %x_ref.1, bf16[512,1024]{1,0:T(8,128)(2,1)} %g_ref.1, bf16[2,128,1024]{2,1,0:T(8,128)(2,1)} %get-tuple-element.26.wi_ref, ...), custom_call_target="tpu_custom_call" | custom-call | tf_op jit(solution)/shard_map/pallas_call | solution.py:368
  196.2 0.0 copy-start.1
  196.2 1.3 reduce
  197.5 0.6 reshape.310
  198.2 0.0 copy-start
  198.2 2.5 %copy.25 = bf16[128,2,1024]{2,1,0:T(2,128)(2,1)} copy(bf16[128,2,1024]{2,0,1:T(8,128)(2,1)} %bitcast.43) | data formatting | bytes 1048576
  200.6 0.0 copy-done.1
  200.6 1.3 copy.26
  202.0 0.0 copy-done
  202.0 1.0 copy.39
  (8 shorter events, 0.1 us)
Async XLA Ops:
  8.1 1.4 copy-start.2
  8.1 1.4 copy-start.3
  196.2 4.4 %copy-start.1 = (bf16[2,128,1024]{2,1,0:T(8,128)(2,1)S(1)}, bf16[2,128,1024]{2,1,0:T(8,128)(2,1)}, u32[]{:S(2)}) copy-start(bf16[2,128,1024]{2,1,0:T(8,128)(2,1)} %get-tuple-element.11) | copy-start | bytes 1572868
  198.2 3.8 %copy-start = (bf16[512,1024]{1,0:T(8,128)(2,1)S(1)}, bf16[512,1024]{1,0:T(8,128)(2,1)}, u32[]{:S(2)}) copy-start(bf16[512,1024]{1,0:T(8,128)(2,1)} %get-tuple-element.31) | copy-start | bytes 3145732

commit v3 on v2

--- a/solution.py
+++ b/solution.py
@@ -38,9 +38,9 @@
 
 def layer_kernel(
     n_peers, n_ring, slots, group, tile,
-    x_ref, g_ref, wi_ref, wo_ref, table_ref, slot_col, slot_row, gate_col,
+    x_ref, g_ref, wi_ref, wo_ref, table_ref, slot_col, gate_col,
     tok_ref, gate_ref, wig_ref, wog_ref,
-    full, send_x, send_g, recv_x, recv_g, recv_b, sel, want,
+    full, send_x, send_g, recv_x, recv_g, recv_b, sel, want, pick,
     picked_x, picked_g, scaled, hidden, slope, pre_grad, in_grad, ring,
     ag_send, ag_recv, rs_send, rs_recv, t_send, t_recv, a_send, a_recv, own_sem,
 ):
@@ -201,6 +201,12 @@
         ag_step(0, 1)
     gather(g_ref, send_g)
     send_all(1, send_g, recv_g)
+
+    def make_pick(i):
+        at = lax.broadcasted_iota(i32, (tile, n_slots), 1)
+        pick[rows_of(i), :] = jnp.where(slot_col[rows_of(i), :] == at, 1.0, 0.0).astype(bf16)
+
+    loop(tiles, make_pick)
     for s in range(2, half):
         ag_step(0, s)
     if half > 1:
@@ -210,34 +216,27 @@
         own_copy(0, e).wait()
     receive_all(0, send_x, recv_x)
 
-    def pick_tile(i):
-        at = lax.broadcasted_iota(i32, (tile, n_slots), 1)
-        return jnp.where(slot_col[rows_of(i), :] == at, 1.0, 0.0).astype(bf16)
-
     def forward(i):
         rows = rows_of(i)
-        picked = dot(pick_tile(i), recv_x[...], 1, 0).astype(bf16)
+        picked = dot(pick[rows, :], recv_x[...], 1, 0).astype(bf16)
         picked_x[rows, :] = picked
         value, grade = gelu_parts(dot(picked, full[0, i // per_expert], 1, 0))
         hidden[rows, :] = value.astype(bf16)
         slope[rows, :] = grade
 
-    loop(tiles, forward)
-    for s in range(2, half + 1):
+    loop(per_expert, forward)
+    if half > 2:
+        ag_step(1, 2)
+    loop(per_expert, lambda i: forward(i + per_expert))
+    for s in range(3, half):
         ag_step(1, s)
-    if half == 1:
-        ag_step(1, 1)
-    for e in range(2):
-        own_copy(1, e).wait()
     receive_all(1, send_g, recv_g)
 
     def arrive_grad(i):
         rows = rows_of(i)
-        grad = dot(pick_tile(i), recv_g[...], 1, 0).astype(bf16)
+        grad = dot(pick[rows, :], recv_g[...], 1, 0).astype(bf16)
         picked_g[rows, :] = grad
         scaled[rows, :] = (gate_col[rows, :] * grad.astype(f32)).astype(bf16)
-
-    loop(tiles, arrive_grad)
 
     def part(m, e, t):
         columns = pl.ds(pl.multiple_of(t * shard, shard), shard)
@@ -259,6 +258,11 @@
             block = block + ring[m, e, d, s].astype(f32)
         ring[m, e, d, s] = block.astype(bf16)
         rs_copy(m, e, d, s).start()
+
+    def rs_first(m, e):
+        rs_hop(m, e, e, 0, half)
+        if half > 1:
+            rs_hop(m, e, 1 - e, 0, half - 1)
 
     def rs_step(m, s):
         loop(2, lambda e: rs_hop(m, e, e, s, half))
@@ -287,25 +291,34 @@
         in_grad[rows, :] = dot(pre_grad[rows, :], full[0, i // per_expert], 1, 1).astype(bf16)
 
     def back(k):
-        at = lax.broadcasted_iota(i32, (span, picks), 0) + k * span
-        place = jnp.where(slot_row[...] == at, 1.0, 0.0).astype(bf16)
         rows = pl.ds(pl.multiple_of(k * span, span), span)
-        send_x[rows, :] = dot(place, in_grad[...], 1, 0).astype(bf16)
+        send_x[rows, :] = dot(pick[:, rows], in_grad[...], 0, 0).astype(bf16)
 
     def gate_part(i):
         rows = rows_of(i)
         wide = dot(hidden[rows, :], full[1, i // per_expert], 1, 0)
         gate_ref[rows, :] = jnp.sum(picked_g[rows, :].astype(f32) * wide, axis=1, keepdims=True)
 
-    rs_step(1, 0)
-    loop(tiles, backward)
-    rs_step(0, 0)
+    def grads_of(e):
+        loop(per_expert, lambda i: arrive_grad(i + e * per_expert))
+        rs_first(1, e)
+
+    def back_of(e):
+        loop(per_expert, lambda i: backward(i + e * per_expert))
+        rs_first(0, e)
+
+    loop(2, grads_of)
+    ag_step(1, half)
+    for e in range(2):
+        own_copy(1, e).wait()
+    loop(2, back_of)
     loop(tiles, to_input)
+    if half > 1:
+        rs_step(1, 1)
     sent_all(0, send_x, recv_x)
     loop(n_peers // group, back)
     send_all(2, send_x, recv_b)
     if half > 1:
-        rs_step(1, 1)
         rs_step(0, 1)
     loop(tiles, gate_part)
     for s in range(2, half):
@@ -373,7 +386,7 @@
             jax.ShapeDtypeStruct((exp_local, shard, hid), bf16),
             jax.ShapeDtypeStruct((exp_local, shard, width), bf16),
         ),
-        in_specs=[vmem] * 8,
+        in_specs=[vmem] * 7,
         out_specs=(vmem,) * 4,
         scratch_shapes=[
             pltpu.VMEM((2, exp_local, width, hid), bf16),
@@ -384,6 +397,7 @@
             pltpu.VMEM(rows, bf16),
             pltpu.VMEM((tok_local, n_slots), bf16),
             pltpu.VMEM((n_peers, 1, group * slots), i32),
+            pltpu.VMEM((picks, n_slots), bf16),
             pltpu.VMEM((picks, width), bf16),
             pltpu.VMEM((picks, width), bf16),
             pltpu.VMEM((picks, width), bf16),
@@ -412,7 +426,6 @@
         w_out.transpose(1, 0, 2),
         table.reshape(n_peers, 1, group * slots),
         slot_of.reshape(picks, 1),
-        slot_of.reshape(1, picks),
         gates,
     )
     return (

time: 203 us -> 199 us (0.980)
  Pallas kernels: 185 us -> 182 us
    pallas_call x1, Pallas kernels: 185 us -> 182 us  [on_device(): pl.pallas_call(functools.partial(layer_kernel, n_peers, n_ring, slots, gr...]
    unnamed x18 -> x20, local copies, waits for them, and re-layouts: 7.72 us -> 7.05 us
where the time goes in v3:
time: 199 us
  Pallas kernels  182 us (91%)
  local copies, waits for them, and re-layouts  9.81 us (5%)
  other arithmetic  4.66 us (2%)
    pallas_call x1, Pallas kernels, on_device(): pl.pallas_call(functools.partial(layer_kernel, n_peers, n_ring, slots, gr...  182 us
    unnamed x20, local copies, waits for them, and re-layouts  7.05 us

profile of v3, /device:TPU:2, one launch (start us, length us, event | category | flops | bytes accessed | tf_op | source)
XLA Modules:
  0.0 198.5 jit_solution(8406241206788889638)
XLA Ops:
  0.6 0.0 copy-start.4
  0.7 0.7 fusion.29
  1.4 0.7 broadcast_compare_fusion
  2.1 0.7 multiply_bitcast_fusion
  2.8 0.7 copy.27
  3.5 0.5 fusion.4
  4.1 0.0 copy-done.4
  4.1 0.5 fusion.3
  4.6 0.7 reshape.201.table_ref
  5.3 0.3 copy.29
  5.5 0.2 copy.31
  5.8 0.2 copy.22
  6.0 0.0 copy-start.2
  6.0 0.0 copy-start.3
  6.0 1.2 fusion.10.slot_col
  7.2 1.0 copy.33
  8.3 0.0 copy-done.2
  8.3 0.0 copy-done.3
  8.3 1.2 copy_bitcast_fusion
  9.5 182.3 %shard_map.102 = (bf16[512,1024]{1,0:T(8,128)(2,1)}, f32[1024,1]{1,0:T(8,128)}, bf16[2,128,1024]{2,1,0:T(8,128)(2,1)}, bf16[2,128,1024]{2,1,0:T(8,128)(2,1)}) custom-call(bf16[512,1024]{1,0:T(8,128)(2,1)} %x_ref.1, bf16[512,1024]{1,0:T(8,128)(2,1)} %g_ref.1, bf16[2,128,1024]{2,1,0:T(8,128)(2,1)} %get-tuple-element.26.wi_ref, ...), custom_call_target="tpu_custom_call" | custom-call | tf_op jit(solution)/shard_map/pallas_call | solution.py:381
  191.8 0.0 copy-start.1
  191.8 1.3 reduce
  193.1 0.6 reshape.204
  193.8 0.0 copy-start
  193.8 2.5 %copy.25 = bf16[128,2,1024]{2,1,0:T(2,128)(2,1)} copy(bf16[128,2,1024]{2,0,1:T(8,128)(2,1)} %bitcast.38) | data formatting | bytes 1048576
  196.2 0.0 copy-done.1
  196.2 1.3 copy.26
  197.6 0.0 copy-done
  197.6 1.0 copy.37
  (9 shorter events, 0.1 us)
Async XLA Ops:
  0.6 3.4 %copy-start.4 = (s32[1,2,512]{2,1,0:T(2,128)S(1)}, s32[1,2,512]{2,1,0:T(2,128)}, u32[]{:S(2)}) copy-start(s32[1,2,512]{2,1,0:T(2,128)} %param.11) | copy-start | bytes 12292
  6.0 2.3 %copy-start.2 = (bf16[128,2,1024]{2,1,0:T(2,128)(2,1)S(1)}, bf16[128,2,1024]{2,1,0:T(2,128)(2,1)}, u32[]{:S(2)}) copy-start(bf16[128,2,1024]{2,1,0:T(2,128)(2,1)} %param.10) | copy-start | bytes 1572868
  6.0 2.2 %copy-start.3 = (bf16[128,2,1024]{2,1,0:T(2,128)(2,1)S(1)}, bf16[128,2,1024]{2,1,0:T(2,128)(2,1)}, u32[]{:S(2)}) copy-start(bf16[128,2,1024]{2,1,0:T(2,128)(2,1)} %param.9) | copy-start | bytes 1572868
  191.8 4.4 %copy-start.1 = (bf16[2,128,1024]{2,1,0:T(8,128)(2,1)S(1)}, bf16[2,128,1024]{2,1,0:T(8,128)(2,1)}, u32[]{:S(2)}) copy-start(bf16[2,128,1024]{2,1,0:T(8,128)(2,1)} %get-tuple-element.11) | copy-start | bytes 1572868
  193.8 3.8 %copy-start = (bf16[512,1024]{1,0:T(8,128)(2,1)S(1)}, bf16[512,1024]{1,0:T(8,128)(2,1)}, u32[]{:S(2)}) copy-start(bf16[512,1024]{1,0:T(8,128)(2,1)} %get-tuple-element.31) | copy-start | bytes 3145732
